TPU v7x, 32 devices: a whole 2x2x4 slice. The times are simulated.
32 devices in a mesh: dp: 16 (over z, x, core), tensor: 2 (over y).
Axes of the slice: x: 2, y: 2, z: 4, core: 2. Of those that a mesh axis runs over, the one named last changes fastest.
Arguments:
- tokens: bfloat16 [4096, 2048], P(('dp', 'tensor')), may hold values from -6 to 6
- segment_ids: int32 [16, 256], P('dp'), may hold values from 0 to 3, never falling along the last dimension, each value on 1 to 128 neighbouring positions
- w_query: bfloat16 [2048, 2048], P('dp', 'tensor'), may hold values from -0.125 to 0.125
- w_key: bfloat16 [2048, 2048], P('dp', 'tensor'), may hold values from -0.125 to 0.125
- w_value: bfloat16 [2048, 2048], P('dp', 'tensor'), may hold values from -0.125 to 0.125
- w_output: bfloat16 [2048, 2048], P('dp', 'tensor'), may hold values from -0.125 to 0.125
- w_gate: bfloat16 [2048, 8192], P('dp', 'tensor'), may hold values from -0.125 to 0.125
- w_up: bfloat16 [2048, 8192], P('dp', 'tensor'), may hold values from -0.125 to 0.125
- w_down: bfloat16 [2048, 8192], P('dp', 'tensor'), may hold values from -0.0625 to 0.0625
- query_gain: float32 [2048], P(('dp', 'tensor')), may hold values from 0.5 to 2
- key_gain: float32 [2048], P(('dp', 'tensor')), may hold values from 0.5 to 2
- attn_gain: float32 [2048], P(('dp', 'tensor')), may hold values from 0.1 to 1.9
- ffn_gain: float32 [2048], P(('dp', 'tensor')), may hold values from 0.1 to 1.9
- cotangent: bfloat16 [4096, 2048], P(('dp', 'tensor')), may hold values from -6 to 6
Outputs:
- output: bfloat16 [4096, 2048], P(('dp', 'tensor'))
- grad_tokens: float32 [4096, 2048], P(('dp', 'tensor'))
- grad_query: float32 [2048, 2048], P('dp', 'tensor')
- grad_key: float32 [2048, 2048], P('dp', 'tensor')
- grad_value: float32 [2048, 2048], P('dp', 'tensor')
- grad_output: float32 [2048, 2048], P('dp', 'tensor')
- grad_gate: float32 [2048, 8192], P('dp', 'tensor')
- grad_up: float32 [2048, 8192], P('dp', 'tensor')
- grad_down: float32 [2048, 8192], P('dp', 'tensor')
- grad_query_gain: float32 [2048], P(('dp', 'tensor'))
- grad_key_gain: float32 [2048], P(('dp', 'tensor'))
- grad_attn_gain: float32 [2048], P(('dp', 'tensor'))
- grad_ffn_gain: float32 [2048], P(('dp', 'tensor'))
Inputs may be any that keep to these rules, and one draw needn't show every extreme that they name: `segment_ids`: within each sequence the ids never fall; each document has 1 to 128 tokens, and one has exactly 128.
All inputs are finite; a program needn't handle non-finite values.
Results may differ from a plain program's by a relative error of at most 0.015.
Values may be sent and summed in bfloat16 or wider, within the bound.
No kernel may reach another device: no remote copies, remote signals or barrier semaphores. Data moves between devices by JAX's collectives and lax.ppermute only.
A program may use at most 384 MiB of HBM per device.

v0:
```python
import math
import jax
import jax.numpy as jnp
from jax import lax
from jax.sharding import PartitionSpec as P

HD = 128
EPSILON = 1e-06
NEGATIVE = -1e30


def rms_scale(values):
    return lax.rsqrt(jnp.mean(values * values, axis=1, keepdims=True) + EPSILON)


def whole_rows(halves):
    return lax.all_gather(halves, "tensor", axis=0, tiled=True)


def to_halves(partial_value):
    return lax.psum_scatter(partial_value, "tensor", scatter_dimension=0, tiled=True)


def norm_totals(pair):
    return lax.psum((pair[0], pair[1]), "tensor")


def shards(
    tokens,
    segment_ids,
    w_query,
    w_key,
    w_value,
    w_output,
    w_gate,
    w_up,
    w_down,
    query_gain,
    key_gain,
    attn_gain,
    ffn_gain,
    cotangent,
):
    tensor_index = lax.axis_index("tensor")
    head_width = w_query.shape[1]
    ffn_width = w_gate.shape[1]
    own_rows = w_query.shape[0]
    model_width = own_rows * lax.axis_size("dp")
    seq_length = tokens.shape[0] * lax.axis_size("tensor")
    local_heads = head_width // HD
    score_scale = 1.0 / math.sqrt(HD)
    gains = lax.all_gather(
        jnp.stack([query_gain, key_gain, attn_gain, ffn_gain]), ("dp", "tensor"), axis=1, tiled=True
    )
    query_scale = lax.dynamic_slice_in_dim(gains[0], tensor_index * head_width, head_width)
    key_scale = lax.dynamic_slice_in_dim(gains[1], tensor_index * head_width, head_width)
    attn_scale = gains[2]
    ffn_scale = gains[3]
    positions = jnp.arange(seq_length)
    seq_ids = segment_ids[0]
    visible = (positions[:, None] >= positions[None, :]) & (seq_ids[:, None] == seq_ids[None, :])
    whole_input = whole_rows(tokens)
    pieces = (
        lax.all_gather(w_query, "dp", axis=0, tiled=True),
        lax.all_gather(w_key, "dp", axis=0, tiled=True),
        lax.all_gather(w_value, "dp", axis=0, tiled=True),
        lax.all_gather(w_output, "dp", axis=0, tiled=True),
    )
    columns = whole_input
    query_acc = jnp.dot(columns, pieces[0], preferred_element_type=jnp.float32)
    key_acc = jnp.dot(columns, pieces[1], preferred_element_type=jnp.float32)
    value_acc = jnp.dot(columns, pieces[2], preferred_element_type=jnp.float32)
    stored = pieces[3]
    query, key_proj, value_acc, output_rows = (query_acc, key_acc, value_acc, stored)
    squares = norm_totals((jnp.sum(query * query, axis=1), jnp.sum(key_proj * key_proj, axis=1)))
    q_rms = lax.rsqrt(squares[0] / model_width + EPSILON)[:, None]
    k_rms = lax.rsqrt(squares[1] / model_width + EPSILON)[:, None]
    normed_query = (query * q_rms * query_scale).astype(jnp.bfloat16)
    normed_key = (key_proj * k_rms * key_scale).astype(jnp.bfloat16)
    value_bf = value_acc.astype(jnp.bfloat16)
    query_heads = normed_query.reshape(seq_length, local_heads, HD)
    key_heads = normed_key.reshape(seq_length, local_heads, HD)
    value_heads = value_bf.reshape(seq_length, local_heads, HD)
    scores = (
        jnp.einsum("qhd,khd->hqk", query_heads, key_heads, preferred_element_type=jnp.float32)
        * score_scale
    )
    scores = jnp.where(visible[None], scores, NEGATIVE)
    peak = jnp.max(scores, axis=-1, keepdims=True)
    expo = jnp.exp(scores - peak)
    total = jnp.sum(expo, axis=-1, keepdims=True)
    log_total = peak + jnp.log(total)
    prob_bf = (expo / total).astype(jnp.bfloat16)
    attn_heads = jnp.einsum(
        "hqk,khd->qhd", prob_bf, value_heads, preferred_element_type=jnp.float32
    ).astype(jnp.bfloat16)
    attn = attn_heads.reshape(seq_length, head_width)
    proj = to_halves(jnp.einsum("sc,oc->so", attn, output_rows, preferred_element_type=jnp.float32))
    attn_rms = rms_scale(proj)
    resid = tokens.astype(jnp.float32) + proj * attn_rms * attn_scale
    whole_hidden = whole_rows(resid.astype(jnp.bfloat16))
    pieces = (
        lax.all_gather(w_gate, "dp", axis=0, tiled=True),
        lax.all_gather(w_up, "dp", axis=0, tiled=True),
        lax.all_gather(w_down, "dp", axis=0, tiled=True),
    )
    columns = whole_hidden
    gate_acc = jnp.dot(columns, pieces[0], preferred_element_type=jnp.float32)
    up_acc = jnp.dot(columns, pieces[1], preferred_element_type=jnp.float32)
    stored = pieces[2]
    sigma = jax.nn.sigmoid(gate_acc)
    act = (gate_acc * sigma * up_acc).astype(jnp.bfloat16)
    ffn = to_halves(jnp.einsum("sf,of->so", act, stored, preferred_element_type=jnp.float32))
    ffn_rms = rms_scale(ffn)
    output = (resid + ffn * ffn_rms * ffn_scale).astype(jnp.bfloat16)
    d_out = cotangent.astype(jnp.float32)
    ffn_gain_term = jnp.sum(d_out * ffn * ffn_rms, axis=0)
    scaled_out = d_out * ffn_scale
    d_ffn = (
        ffn_rms
        * (scaled_out - ffn * ffn_rms * ffn_rms * jnp.mean(scaled_out * ffn, axis=1, keepdims=True))
    ).astype(jnp.bfloat16)
    whole_dffn = whole_rows(d_ffn)
    d_act = jnp.dot(whole_dffn, stored, preferred_element_type=jnp.float32)
    d_gate = (d_act * up_acc * sigma * (1.0 + gate_acc * (1.0 - sigma))).astype(jnp.bfloat16)
    d_up = (d_act * gate_acc * sigma).astype(jnp.bfloat16)
    pieces = (
        lax.all_gather(w_gate, "dp", axis=0, tiled=True),
        lax.all_gather(w_up, "dp", axis=0, tiled=True),
    )
    block = jnp.einsum(
        "sf,rf->sr", d_gate, pieces[0], preferred_element_type=jnp.float32
    ) + jnp.einsum("sf,rf->sr", d_up, pieces[1], preferred_element_type=jnp.float32)
    hidden_part = block
    d_resid = d_out + to_halves(hidden_part)
    attn_gain_term = jnp.sum(d_resid * proj * attn_rms, axis=0)
    scaled_resid = d_resid * attn_scale
    d_proj = (
        attn_rms
        * (
            scaled_resid
            - proj * attn_rms * attn_rms * jnp.mean(scaled_resid * proj, axis=1, keepdims=True)
        )
    ).astype(jnp.bfloat16)
    whole_dproj = whole_rows(d_proj)
    d_attn = jnp.dot(whole_dproj, output_rows, preferred_element_type=jnp.float32).astype(
        jnp.bfloat16
    )
    d_attn_heads = d_attn.reshape(seq_length, local_heads, HD)
    back_prob = jnp.where(visible[None], jnp.exp(scores - log_total), 0.0)
    back_bf = back_prob.astype(jnp.bfloat16)
    d_value = (
        jnp.einsum("hqk,qhd->khd", back_bf, d_attn_heads, preferred_element_type=jnp.float32)
        .reshape(seq_length, head_width)
        .astype(jnp.bfloat16)
    )
    d_prob = jnp.einsum(
        "qhd,khd->hqk", d_attn_heads, value_heads, preferred_element_type=jnp.float32
    )
    delta = jnp.einsum("qhd,qhd->hq", d_attn_heads, attn_heads, preferred_element_type=jnp.float32)[
        ..., None
    ]
    d_score = (back_prob * (d_prob - delta)).astype(jnp.bfloat16)
    d_nq = (
        jnp.einsum("hqk,khd->qhd", d_score, key_heads, preferred_element_type=jnp.float32).reshape(
            seq_length, head_width
        )
        * score_scale
    )
    d_nk = (
        jnp.einsum(
            "hqk,qhd->khd", d_score, query_heads, preferred_element_type=jnp.float32
        ).reshape(seq_length, head_width)
        * score_scale
    )
    query_gain_term = jnp.sum(d_nq * query * q_rms, axis=0)
    key_gain_term = jnp.sum(d_nk * key_proj * k_rms, axis=0)
    scaled_q = d_nq * query_scale
    scaled_k = d_nk * key_scale
    inner = norm_totals((jnp.sum(scaled_q * query, axis=1), jnp.sum(scaled_k * key_proj, axis=1)))
    d_query = (
        q_rms * (scaled_q - query * q_rms * q_rms * (inner[0] / model_width)[:, None])
    ).astype(jnp.bfloat16)
    d_key = (
        k_rms * (scaled_k - key_proj * k_rms * k_rms * (inner[1] / model_width)[:, None])
    ).astype(jnp.bfloat16)
    pieces = (
        lax.all_gather(w_query, "dp", axis=0, tiled=True),
        lax.all_gather(w_key, "dp", axis=0, tiled=True),
        lax.all_gather(w_value, "dp", axis=0, tiled=True),
    )
    block = (
        jnp.einsum("sc,rc->sr", d_query, pieces[0], preferred_element_type=jnp.float32)
        + jnp.einsum("sc,rc->sr", d_key, pieces[1], preferred_element_type=jnp.float32)
        + jnp.einsum("sc,rc->sr", d_value, pieces[2], preferred_element_type=jnp.float32)
    )
    grad_tokens = d_resid + to_halves(block)
    gate_term = jnp.einsum("sr,sf->rf", whole_hidden, d_gate, preferred_element_type=jnp.float32)
    up_term = jnp.einsum("sr,sf->rf", whole_hidden, d_up, preferred_element_type=jnp.float32)
    down_term = jnp.einsum("sr,sf->rf", whole_dffn, act, preferred_element_type=jnp.float32)
    query_term = jnp.einsum("sr,sc->rc", whole_input, d_query, preferred_element_type=jnp.float32)
    key_term = jnp.einsum("sr,sc->rc", whole_input, d_key, preferred_element_type=jnp.float32)
    value_term = jnp.einsum("sr,sc->rc", whole_input, d_value, preferred_element_type=jnp.float32)
    output_term = jnp.einsum("sr,sc->rc", whole_dproj, attn, preferred_element_type=jnp.float32)
    combined = lax.psum_scatter(
        jnp.concatenate(
            [
                jnp.concatenate([query_term, key_term, value_term, output_term], axis=1),
                jnp.concatenate([gate_term, up_term, down_term], axis=1),
            ],
            axis=1,
        ),
        "dp",
        scatter_dimension=0,
        tiled=True,
    )
    attn_sums = combined[:, : 4 * head_width]
    mlp_sums = combined[:, 4 * head_width :]
    gain_zero = jnp.zeros((model_width,), jnp.float32)
    query_placed = lax.dynamic_update_slice_in_dim(
        gain_zero, query_gain_term, tensor_index * head_width, 0
    )
    key_placed = lax.dynamic_update_slice_in_dim(
        gain_zero, key_gain_term, tensor_index * head_width, 0
    )
    gain_parts = lax.psum_scatter(
        jnp.stack([query_placed, key_placed, attn_gain_term, ffn_gain_term]),
        ("dp", "tensor"),
        scatter_dimension=1,
        tiled=True,
    )
    grad_query = attn_sums[:, :head_width]
    grad_key = attn_sums[:, head_width : 2 * head_width]
    grad_value = attn_sums[:, 2 * head_width : 3 * head_width]
    grad_output = attn_sums[:, 3 * head_width :]
    grad_gate = mlp_sums[:, :ffn_width]
    grad_up = mlp_sums[:, ffn_width : 2 * ffn_width]
    grad_down = mlp_sums[:, 2 * ffn_width :]
    return (
        output,
        grad_tokens,
        grad_query,
        grad_key,
        grad_value,
        grad_output,
        grad_gate,
        grad_up,
        grad_down,
        gain_parts[0],
        gain_parts[1],
        gain_parts[2],
        gain_parts[3],
    )


def solution(mesh):
    return jax.shard_map(
        shards,
        mesh=mesh,
        in_specs=(
            P(("dp", "tensor"), None),
            P("dp", None),
            P("dp", "tensor"),
            P("dp", "tensor"),
            P("dp", "tensor"),
            P("dp", "tensor"),
            P("dp", "tensor"),
            P("dp", "tensor"),
            P("dp", "tensor"),
            P(("dp", "tensor")),
            P(("dp", "tensor")),
            P(("dp", "tensor")),
            P(("dp", "tensor")),
            P(("dp", "tensor"), None),
        ),
        out_specs=(
            P(("dp", "tensor"), None),
            P(("dp", "tensor"), None),
            P("dp", "tensor"),
            P("dp", "tensor"),
            P("dp", "tensor"),
            P("dp", "tensor"),
            P("dp", "tensor"),
            P("dp", "tensor"),
            P("dp", "tensor"),
            P(("dp", "tensor")),
            P(("dp", "tensor")),
            P(("dp", "tensor")),
            P(("dp", "tensor")),
        ),
        check_vma=False,
    )
```

profile of v0, /device:TPU:0, one launch (start us, length us, event | category | flops | bytes accessed | tf_op | source)
XLA Modules:
  0.0 2323.6 jit_solution(9547360384983591995)
XLA Ops:
  11.3 71.0 %all-gather = f32[32,64,4]{1,2,0:T(4,128)S(1)} all-gather(f32[1,64,4]{1,2,0:T(4,128)S(1)} %maximum_bitcast_fusion), channel_id=1, replica_groups=mesh['dp'=16,'tensor'=2] {'dp','tensor'}, dimensions={0}, use_global_device_ids=true | all-gather | bytes 33792 | tf_op jit(solution)/shard_map/all_gather | solution.py:52
  90.3 47.3 %all-gather.19.cloned.1.call-done = bf16[2048,1024]{1,0:T(8,128)(2,1)} async-done(((bf16[128,1024]{1,0:T(8,128)(2,1)}), bf16[2048,1024]{1,0:T(8,128)(2,1)}) %all-gather.19.cloned.1.call-update) | async-done | bytes 4194320 | tf_op jit(solution)/shard_map/all_gather | solution.py:65
  152.3 36.3 %all-gather.15.cloned.1.call-done = bf16[2048,1024]{1,0:T(8,128)(2,1)} async-done(((bf16[128,1024]{1,0:T(8,128)(2,1)}), bf16[2048,1024]{1,0:T(8,128)(2,1)}) %all-gather.15.cloned.1.call-update) | async-done | bytes 4194320 | tf_op jit(solution)/shard_map/all_gather | solution.py:66
  193.4 46.1 %all-gather.21.cloned.1.call-done = bf16[2048,1024]{1,0:T(8,128)(2,1)} async-done(((bf16[128,1024]{1,0:T(8,128)(2,1)}), bf16[2048,1024]{1,0:T(8,128)(2,1)}) %all-gather.21.cloned.1.call-update) | async-done | bytes 4194320 | tf_op jit(solution)/shard_map/all_gather | solution.py:67
  244.5 30.5 %reduce-scatter.9.cloned.1.call-done = f32[128,2048]{1,0:T(8,128)} async-done(((f32[256,2048]{1,0:T(8,128)}), f32[128,2048]{1,0:T(8,128)}) %reduce-scatter.9.cloned.1.call-update) | async-done | bytes 1048592 | tf_op jit(solution)/shard_map/reduce_scatter | solution.py:21
  281.0 19.1 all-gather.23.cloned.1.call-done
  300.1 128.6 %all-gather.25.cloned.1.call-done = bf16[2048,4096]{1,0:T(8,128)(2,1)} async-done(((bf16[128,4096]{1,0:T(8,128)(2,1)}), bf16[2048,4096]{1,0:T(8,128)(2,1)}) %all-gather.25.cloned.1.call-update) | async-done | bytes 16777232 | tf_op jit(solution)/shard_map/all_gather | solution.py:103
  428.8 12.6 fusion.29
  441.3 114.2 %all-gather.27.cloned.1.call-done = bf16[2048,4096]{1,0:T(8,128)(2,1)} async-done(((bf16[128,4096]{1,0:T(8,128)(2,1)}), bf16[2048,4096]{1,0:T(8,128)(2,1)}) %all-gather.27.cloned.1.call-update) | async-done | bytes 16777232 | tf_op jit(solution)/shard_map/all_gather | solution.py:104
  555.6 13.4 multiply_convert_fusion.2
  569.0 113.2 %all-gather.29.cloned.1.call-done = bf16[2048,4096]{1,0:T(8,128)(2,1)} async-done(((bf16[128,4096]{1,0:T(8,128)(2,1)}), bf16[2048,4096]{1,0:T(8,128)(2,1)}) %all-gather.29.cloned.1.call-update) | async-done | bytes 16777232 | tf_op jit(solution)/shard_map/all_gather | solution.py:105
  682.2 12.3 fusion.30
  694.6 30.2 %reduce-scatter.11.cloned.1.call-done = f32[128,2048]{1,0:T(8,128)} async-done(((f32[256,2048]{1,0:T(8,128)}), f32[128,2048]{1,0:T(8,128)}) %reduce-scatter.11.cloned.1.call-update) | async-done | bytes 1048592 | tf_op jit(solution)/shard_map/reduce_scatter | solution.py:21
  730.3 21.2 all-gather.31.cloned.1.call-done
  751.5 16.0 multiply_convert_fusion
  779.7 13.3 convolution_add_fusion.2
  793.0 32.0 %reduce-scatter.13.cloned.1.call-done = f32[128,2048]{1,0:T(8,128)} async-done(((f32[256,2048]{1,0:T(8,128)}), f32[128,2048]{1,0:T(8,128)}) %reduce-scatter.13.cloned.1.call-update) | async-done | bytes 1048592 | tf_op jit(solution)/shard_map/reduce_scatter | solution.py:21
  830.2 21.4 all-gather.33.cloned.1.call-done
  959.2 13.3 convolution_dynamic-update-slice_fusion.2
  972.5 13.2 convolution_dynamic-update-slice_fusion.1
  985.7 13.2 convolution_dynamic-update-slice_fusion
  999.0 36.0 %reduce-scatter.19.cloned.1.call-done = f32[64,4]{1,0:T(8,128)} async-done(((f32[2048,4]{1,0:T(8,128)}), f32[64,4]{1,0:T(8,128)}) %reduce-scatter.19.cloned.1.call-update) | async-done | bytes 1040
  1038.3 26.8 %reduce-scatter.15.cloned.1.call-done = f32[128,2048]{1,0:T(8,128)} async-done(((f32[256,2048]{1,0:T(8,128)}), f32[128,2048]{1,0:T(8,128)}) %reduce-scatter.15.cloned.1.call-update) | async-done | bytes 1048592 | tf_op jit(solution)/shard_map/reduce_scatter | solution.py:21
  1067.4 1240.7 %reduce-scatter.17.cloned.1.call-done = f32[128,16384]{1,0:T(8,128)} async-done(((f32[2048,16384]{1,0:T(8,128)}), f32[128,16384]{1,0:T(8,128)}) %reduce-scatter.17.cloned.1.call-update) | async-done | bytes 8388624 | tf_op jit(solution)/shard_map/reduce_scatter | solution.py:205
  (181 shorter events, 187.0 us)
Async XLA Ops:
  7.2 76.2 %all-gather.13.cloned.1.call-start = ((), (), s32[]{:S(2)}) async-start(), calls=%async_computation.6 | async-start | bytes 1572864 | tf_op jit(solution)/shard_map/all_gather | solution.py:17
  7.9 78.5 %all-gather.17.cloned.1.call-start = ((), (), s32[]{:S(2)}) async-start(), calls=%async_computation.8 | async-start | bytes 4456448 | tf_op jit(solution)/shard_map/all_gather | solution.py:64
  8.7 129.0 %all-gather.19.cloned.1.call-start = ((), (), s32[]{:S(2)}) async-start(), calls=%async_computation.9 | async-start | bytes 4456448 | tf_op jit(solution)/shard_map/all_gather | solution.py:65
  9.4 179.2 %all-gather.15.cloned.1.call-start = ((), (), s32[]{:S(2)}) async-start(), calls=%async_computation.7 | async-start | bytes 4456448 | tf_op jit(solution)/shard_map/all_gather | solution.py:66
  10.0 229.6 %all-gather.21.cloned.1.call-start = ((), (), s32[]{:S(2)}) async-start(), calls=%async_computation.10 | async-start | bytes 4456448 | tf_op jit(solution)/shard_map/all_gather | solution.py:67
  10.6 264.5 %reduce-scatter.9.cloned.1.call-start = ((), (), s32[]{:S(2)}) async-start(), calls=%async_computation.11 | async-start | bytes 3145728 | tf_op jit(solution)/shard_map/reduce_scatter | solution.py:21
  83.4 54.2 %copy-start.4 = (bf16[256,2048]{1,0:T(8,128)(2,1)S(1)}, bf16[256,2048]{1,0:T(8,128)(2,1)}, u32[]{:S(2)}) copy-start(bf16[256,2048]{1,0:T(8,128)(2,1)} %all-gather.13.cloned.1.call-done) | copy-start | bytes 3145732
  90.3 56.8 %copy-start.8 = (f32[256,1024]{1,0:T(8,128)}, f32[256,1024]{1,0:T(8,128)S(1)}, u32[]{:S(2)}) copy-start(f32[256,1024]{1,0:T(8,128)S(1)} %get-tuple-element.45) | copy-start | bytes 3145732
  193.4 51.0 %copy-start.23 = (bf16[8,128,256]{2,1,0:T(8,128)(2,1)}, bf16[8,128,256]{2,1,0:T(8,128)(2,1)S(1)}, u32[]{:S(2)}) copy-start(bf16[8,128,256]{2,1,0:T(8,128)(2,1)S(1)} %convolution_convert_fusion.1) | copy-start | bytes 1572868
  244.4 55.7 %all-gather.23.cloned.1.call-start = ((), (), s32[]{:S(2)}) async-start(), calls=%async_computation.12 | async-start | bytes 1572864 | tf_op jit(solution)/shard_map/all_gather | solution.py:17
  278.7 150.1 %all-gather.25.cloned.1.call-start = ((), (), s32[]{:S(2)}) async-start(), calls=%async_computation.13 | async-start | bytes 17825792 | tf_op jit(solution)/shard_map/all_gather | solution.py:103
  279.5 276.1 %all-gather.27.cloned.1.call-start = ((), (), s32[]{:S(2)}) async-start(), calls=%async_computation.14 | async-start | bytes 17825792 | tf_op jit(solution)/shard_map/all_gather | solution.py:104
  280.2 402.0 %all-gather.29.cloned.1.call-start = ((), (), s32[]{:S(2)}) async-start(), calls=%async_computation.15 | async-start | bytes 17825792 | tf_op jit(solution)/shard_map/all_gather | solution.py:105
  280.8 444.0 %reduce-scatter.11.cloned.1.call-start = ((), (), s32[]{:S(2)}) async-start(), calls=%async_computation.16 | async-start | bytes 3145728 | tf_op jit(solution)/shard_map/reduce_scatter | solution.py:21
  300.1 255.4 %copy-start.13 = (bf16[256,2048]{1,0:T(8,128)(2,1)S(1)}, bf16[256,2048]{1,0:T(8,128)(2,1)}, u32[]{:S(2)}) copy-start(bf16[256,2048]{1,0:T(8,128)(2,1)} %all-gather.23.cloned.1.call-done) | copy-start | bytes 3145732
  694.5 57.0 %all-gather.31.cloned.1.call-start = ((), (), s32[]{:S(2)}) async-start(), calls=%async_computation.17 | async-start | bytes 1572864 | tf_op jit(solution)/shard_map/all_gather | solution.py:17
  730.1 94.9 %reduce-scatter.13.cloned.1.call-start = ((), (), s32[]{:S(2)}) async-start(), calls=%async_computation.18 | async-start | bytes 3145728 | tf_op jit(solution)/shard_map/reduce_scatter | solution.py:21
  779.7 45.3 %copy-start.1 = (f32[128,2048]{1,0:T(8,128)S(1)}, f32[128,2048]{1,0:T(8,128)}, u32[]{:S(2)}) copy-start(f32[128,2048]{1,0:T(8,128)} %reduce-scatter.9.cloned.1.call-done) | copy-start | bytes 3145732
  793.0 58.6 %all-gather.33.cloned.1.call-start = ((), (), s32[]{:S(2)}) async-start(), calls=%async_computation.19 | async-start | bytes 1572864 | tf_op jit(solution)/shard_map/all_gather | solution.py:17
  830.1 204.8 %reduce-scatter.19.cloned.1.call-start = ((), (), s32[]{:S(2)}) async-start(), calls=%async_computation.22 | async-start | bytes 1081344
  897.9 167.2 %reduce-scatter.15.cloned.1.call-start = ((), (), s32[]{:S(2)}) async-start(), calls=%async_computation.20 | async-start | bytes 3145728 | tf_op jit(solution)/shard_map/reduce_scatter | solution.py:21
  941.5 1366.6 %reduce-scatter.17.cloned.1.call-start = ((), (), s32[]{:S(2)}) async-start(), calls=%async_computation.21 | async-start | bytes 142606336 | tf_op jit(solution)/shard_map/reduce_scatter | solution.py:205
  999.0 66.1 %copy-start.3 = (bf16[128,2048]{1,0:T(8,128)(2,1)S(1)}, bf16[128,2048]{1,0:T(8,128)(2,1)}, u32[]{:S(2)}) copy-start(bf16[128,2048]{1,0:T(8,128)(2,1)} %param.27) | copy-start | bytes 1572868
  999.0 66.1 %copy-start.10 = (f32[128,2048]{1,0:T(8,128)S(1)}, f32[128,2048]{1,0:T(8,128)}, u32[]{:S(2)}) copy-start(f32[128,2048]{1,0:T(8,128)} %reduce-scatter.13.cloned.1.call-done) | copy-start | bytes 3145732
  (25 other events, 223.7 us)
Sparse Core Ops, SparseCore 0:
  9.5 24.2 all-gather.12
  36.0 50.3 all-gather.16
  88.6 48.9 all-gather.18
  139.6 48.8 all-gather.14
  190.6 48.8 all-gather.20
  244.6 30.4 reduce-scatter.8
  278.8 21.2 all-gather.22
  302.3 126.4 all-gather.24
  430.9 124.5 all-gather.26
  557.6 124.5 all-gather.28
  694.7 30.0 reduce-scatter.10
  730.2 21.2 all-gather.30
  793.1 31.8 reduce-scatter.12
  830.2 21.2 all-gather.32
  898.0 136.8 reduce-scatter.18
  1037.0 27.9 reduce-scatter.14
  1069.2 1238.9 reduce-scatter.16
where the time goes:
time: 2330 us; the launch traced here: 2320 us
  waiting for transfers between devices  1950 us (84%)
  matrix products  173 us (7%)
  blocking collectives  80.9 us (3%)
  local copies, waits for them, and re-layouts  74.9 us (3%)
  other arithmetic  27.1 us (1%)
    reduce_scatter x1, waiting for transfers between devices, shards(): lax.psum_scatter(jnp.concatenate([jnp.concatenate([query_term, key_term,...  1240 us
    all_gather x1, waiting for transfers between devices, shards(): lax.all_gather(w_gate, 'dp', axis=0, tiled=True)  129 us
    reduce_scatter x4, waiting for transfers between devices, to_halves(): lax.psum_scatter(partial_value, 'tensor', scatter_dimension=0, tiled=True)  120 us
    all_gather x1, waiting for transfers between devices, shards(): lax.all_gather(w_up, 'dp', axis=0, tiled=True)  114 us
    all_gather x1, waiting for transfers between devices, shards(): lax.all_gather(w_down, 'dp', axis=0, tiled=True)  113 us
    all_gather x1, blocking collectives, shards(): lax.all_gather(jnp.stack([query_gain, key_gain, attn_gain, ffn_gain]), ('...  71 us
    all_gather x4, waiting for transfers between devices, whole_rows(): return lax.all_gather(halves, 'tensor', axis=0, tiled=True)  61.7 us
    all_gather x1, waiting for transfers between devices, shards(): lax.all_gather(w_key, 'dp', axis=0, tiled=True)  47.3 us
  transfers between devices with their start and end apart: 17, of which 16 were waited for; matrix products, arithmetic and copies ran while one was open for 7% of the time, Pallas kernels for 0%

commit v1 on v0

--- a/solution.py
+++ b/solution.py
@@ -7,6 +7,28 @@
 HD = 128
 EPSILON = 1e-06
 NEGATIVE = -1e30
+
+
+def laid_out(parts, dim):
+    parts = jnp.moveaxis(parts, 0, dim)
+    shape = parts.shape
+    return parts.reshape(*shape[:dim], shape[dim] * shape[dim + 1], *shape[dim + 2 :])
+
+
+def gather_around(x, axis, dim):
+    size = lax.axis_size(axis)
+    pairs = [(i, (i + 1) % size) for i in range(size)]
+    back = [(b, a) for a, b in pairs]
+    lower, upper = ([], [])
+    for step in range(size - 1):
+        if step % 2 == 0:
+            lower.append(lax.ppermute(lower[-1] if lower else x, axis, pairs))
+        else:
+            upper.append(lax.ppermute(upper[-1] if upper else x, axis, back))
+    blocks = jnp.stack([*lower[::-1], x, *upper])
+    shift = lax.axis_index(axis) - len(lower)
+    blocks = blocks[(jnp.arange(size) - shift) % size]
+    return laid_out(blocks, dim)
 
 
 def rms_scale(values):
@@ -100,7 +122,7 @@
     resid = tokens.astype(jnp.float32) + proj * attn_rms * attn_scale
     whole_hidden = whole_rows(resid.astype(jnp.bfloat16))
     pieces = (
-        lax.all_gather(w_gate, "dp", axis=0, tiled=True),
+        gather_around(w_gate, "dp", 0),
         lax.all_gather(w_up, "dp", axis=0, tiled=True),
         lax.all_gather(w_down, "dp", axis=0, tiled=True),
     )

time: 2330 us -> 2400 us (1.030)
  starting transfers between devices: 1.45 us -> 98.2 us
  waiting for transfers between devices: 1950 us -> 1880 us
  local copies, waits for them, and re-layouts: 74.9 us -> 112 us
    ppermute x0 -> x15, waiting for transfers between devices: none -> 137 us  [the longest x8 120 us: gather_around(): lower.append(lax.ppermute(lower[-1] if lower else x, axis, pairs))]
    all_gather x1, waiting for transfers between devices: 114 us -> 0.01 us  [shards(): lax.all_gather(w_up, 'dp', axis=0, tiled=True)]
    ppermute x0 -> x15, starting transfers between devices: none -> 96.6 us  [the longest x8 78.5 us: gather_around(): lower.append(lax.ppermute(lower[-1] if lower else x, axis, pairs))]
    all_gather x1, waiting for transfers between devices: 113 us -> 60.5 us  [shards(): lax.all_gather(w_down, 'dp', axis=0, tiled=True)]
    unnamed x75 -> x128, local copies, waits for them, and re-layouts: 28.4 us -> 51.5 us
  transfers between devices with their start and end apart: 17 -> 32, of which waited for: 16 -> 24; matrix products, arithmetic and copies ran while one was open for 7% -> 9% of each run, Pallas kernels for 0% -> 0%
where the time goes in v1:
time: 2400 us; the launch traced here: 2390 us
  waiting for transfers between devices  1880 us (78%)
  matrix products  174 us (7%)
  local copies, waits for them, and re-layouts  112 us (5%)
  starting transfers between devices  98.2 us (4%)
  blocking collectives  80.9 us (3%)
  other arithmetic  27.1 us (1%)
    reduce_scatter x1, waiting for transfers between devices, shards(): lax.psum_scatter(jnp.concatenate([jnp.concatenate([query_term, key_term,...  1240 us
    ppermute x8, waiting for transfers between devices, gather_around(): lower.append(lax.ppermute(lower[-1] if lower else x, axis, pairs))  120 us
    reduce_scatter x4, waiting for transfers between devices, to_halves(): lax.psum_scatter(partial_value, 'tensor', scatter_dimension=0, tiled=True)  118 us
    all_gather x1, waiting for transfers between devices, shards(): lax.all_gather(w_gate, 'dp', axis=0, tiled=True)  113 us
    ppermute x8, starting transfers between devices, gather_around(): lower.append(lax.ppermute(lower[-1] if lower else x, axis, pairs))  78.5 us
    all_gather x1, blocking collectives, shards(): lax.all_gather(jnp.stack([query_gain, key_gain, attn_gain, ffn_gain]), ('...  71 us
    all_gather x1, waiting for transfers between devices, shards(): lax.all_gather(w_down, 'dp', axis=0, tiled=True)  60.5 us
    unnamed x128, local copies, waits for them, and re-layouts  51.5 us
  transfers between devices with their start and end apart: 32, of which 24 were waited for; matrix products, arithmetic and copies ran while one was open for 9% of the time, Pallas kernels for 0%

profile of v1, /device:TPU:0, one launch (start us, length us, event | category | flops | bytes accessed | tf_op | source)
XLA Modules:
  0.0 2389.5 jit_solution(10581452859004658294)
XLA Ops:
  11.3 71.0 %all-gather = f32[32,64,4]{1,2,0:T(4,128)S(1)} all-gather(f32[1,64,4]{1,2,0:T(4,128)S(1)} %maximum_bitcast_fusion), channel_id=1, replica_groups=mesh['dp'=16,'tensor'=2] {'dp','tensor'}, dimensions={0}, use_global_device_ids=true | all-gather | bytes 33792 | tf_op jit(solution)/shard_map/all_gather | solution.py:74
  90.3 47.3 %all-gather.19.cloned.1.call-done = bf16[2048,1024]{1,0:T(8,128)(2,1)} async-done(((bf16[128,1024]{1,0:T(8,128)(2,1)}), bf16[2048,1024]{1,0:T(8,128)(2,1)}) %all-gather.19.cloned.1.call-update) | async-done | bytes 4194320 | tf_op jit(solution)/shard_map/all_gather | solution.py:87
  152.3 36.3 %all-gather.15.cloned.1.call-done = bf16[2048,1024]{1,0:T(8,128)(2,1)} async-done(((bf16[128,1024]{1,0:T(8,128)(2,1)}), bf16[2048,1024]{1,0:T(8,128)(2,1)}) %all-gather.15.cloned.1.call-update) | async-done | bytes 4194320 | tf_op jit(solution)/shard_map/all_gather | solution.py:88
  193.4 46.1 %all-gather.21.cloned.1.call-done = bf16[2048,1024]{1,0:T(8,128)(2,1)} async-done(((bf16[128,1024]{1,0:T(8,128)(2,1)}), bf16[2048,1024]{1,0:T(8,128)(2,1)}) %all-gather.21.cloned.1.call-update) | async-done | bytes 4194320 | tf_op jit(solution)/shard_map/all_gather | solution.py:89
  244.5 30.5 %reduce-scatter.9.cloned.1.call-done = f32[128,2048]{1,0:T(8,128)} async-done(((f32[256,2048]{1,0:T(8,128)}), f32[128,2048]{1,0:T(8,128)}) %reduce-scatter.9.cloned.1.call-update) | async-done | bytes 1048592 | tf_op jit(solution)/shard_map/reduce_scatter | solution.py:43
  280.3 17.1 collective-permute-done
  314.5 16.1 collective-permute-start.2
  331.5 22.5 collective-permute-done.2
  401.0 14.5 collective-permute-done.4
  415.5 22.4 collective-permute-start.5
  440.2 30.5 %collective-permute-start.6 = (bf16[128,4096]{1,0:T(8,128)(2,1)S(1)}, bf16[128,4096]{1,0:T(8,128)(2,1)}, u32[]{:S(2)}, u32[]{:S(2)}) collective-permute-start(bf16[128,4096]{1,0:T(8,128)(2,1)S(1)} %collective-permute-done.5), channel_id=1, source_target_pairs={{0,2},{2,4},{4,6},{6,8},{8,10},{10,12},{12,14},{14,16},{16,18},{18... | collective-permute-start | bytes 3145736 | tf_op jit(solution)/shard_map/ppermute | solution.py:25
  470.8 27.7 %collective-permute-done.6 = bf16[128,4096]{1,0:T(8,128)(2,1)} collective-permute-done((bf16[128,4096]{1,0:T(8,128)(2,1)S(1)}, bf16[128,4096]{1,0:T(8,128)(2,1)}, u32[]{:S(2)}, u32[]{:S(2)}) %collective-permute-start.6) | collective-permute-done | bytes 1048608 | tf_op jit(solution)/shard_map/ppermute | solution.py:25
  537.9 13.4 gather_fusion
  564.0 14.9 multiply_convert_fusion.2
  578.9 60.5 %all-gather.27.cloned.1.call-done = bf16[2048,4096]{1,0:T(8,128)(2,1)} async-done(((bf16[128,4096]{1,0:T(8,128)(2,1)}), bf16[2048,4096]{1,0:T(8,128)(2,1)}) %all-gather.27.cloned.1.call-update) | async-done | bytes 16777232 | tf_op jit(solution)/shard_map/all_gather | solution.py:127
  651.8 30.2 %reduce-scatter.11.cloned.1.call-done = f32[128,2048]{1,0:T(8,128)} async-done(((f32[256,2048]{1,0:T(8,128)}), f32[128,2048]{1,0:T(8,128)}) %reduce-scatter.11.cloned.1.call-update) | async-done | bytes 1048592 | tf_op jit(solution)/shard_map/reduce_scatter | solution.py:43
  688.3 20.4 all-gather.29.cloned.1.call-done
  708.7 16.0 multiply_convert_fusion
  724.6 112.5 %all-gather.31.cloned.1.call-done = bf16[2048,4096]{1,0:T(8,128)(2,1)} async-done(((bf16[128,4096]{1,0:T(8,128)(2,1)}), bf16[2048,4096]{1,0:T(8,128)(2,1)}) %all-gather.31.cloned.1.call-update) | async-done | bytes 16777232 | tf_op jit(solution)/shard_map/all_gather | solution.py:150
  862.6 30.2 %reduce-scatter.13.cloned.1.call-done = f32[128,2048]{1,0:T(8,128)} async-done(((f32[256,2048]{1,0:T(8,128)}), f32[128,2048]{1,0:T(8,128)}) %reduce-scatter.13.cloned.1.call-update) | async-done | bytes 1048592 | tf_op jit(solution)/shard_map/reduce_scatter | solution.py:43
  898.0 21.3 all-gather.33.cloned.1.call-done
  1066.9 35.4 %reduce-scatter.19.cloned.1.call-done = f32[64,4]{1,0:T(8,128)} async-done(((f32[2048,4]{1,0:T(8,128)}), f32[64,4]{1,0:T(8,128)}) %reduce-scatter.19.cloned.1.call-update) | async-done | bytes 1040
  1105.6 26.7 %reduce-scatter.15.cloned.1.call-done = f32[128,2048]{1,0:T(8,128)} async-done(((f32[256,2048]{1,0:T(8,128)}), f32[128,2048]{1,0:T(8,128)}) %reduce-scatter.15.cloned.1.call-update) | async-done | bytes 1048592 | tf_op jit(solution)/shard_map/reduce_scatter | solution.py:43
  1134.7 1239.2 %reduce-scatter.17.cloned.1.call-done = f32[128,16384]{1,0:T(8,128)} async-done(((f32[2048,16384]{1,0:T(8,128)}), f32[128,16384]{1,0:T(8,128)}) %reduce-scatter.17.cloned.1.call-update) | async-done | bytes 8388624 | tf_op jit(solution)/shard_map/reduce_scatter | solution.py:227
  (268 shorter events, 371.9 us)
Async XLA Ops:
  7.2 76.2 %all-gather.13.cloned.1.call-start = ((), (), s32[]{:S(2)}) async-start(), calls=%async_computation.6 | async-start | bytes 1572864 | tf_op jit(solution)/shard_map/all_gather | solution.py:39
  7.9 78.5 %all-gather.17.cloned.1.call-start = ((), (), s32[]{:S(2)}) async-start(), calls=%async_computation.8 | async-start | bytes 4456448 | tf_op jit(solution)/shard_map/all_gather | solution.py:86
  8.7 129.0 %all-gather.19.cloned.1.call-start = ((), (), s32[]{:S(2)}) async-start(), calls=%async_computation.9 | async-start | bytes 4456448 | tf_op jit(solution)/shard_map/all_gather | solution.py:87
  9.4 179.2 %all-gather.15.cloned.1.call-start = ((), (), s32[]{:S(2)}) async-start(), calls=%async_computation.7 | async-start | bytes 4456448 | tf_op jit(solution)/shard_map/all_gather | solution.py:88
  10.0 229.6 %all-gather.21.cloned.1.call-start = ((), (), s32[]{:S(2)}) async-start(), calls=%async_computation.10 | async-start | bytes 4456448 | tf_op jit(solution)/shard_map/all_gather | solution.py:89
  10.6 264.5 %reduce-scatter.9.cloned.1.call-start = ((), (), s32[]{:S(2)}) async-start(), calls=%async_computation.11 | async-start | bytes 3145728 | tf_op jit(solution)/shard_map/reduce_scatter | solution.py:43
  244.4 306.9 %all-gather.23.cloned.1.call-start = ((), (), s32[]{:S(2)}) async-start(), calls=%async_computation.12 | async-start | bytes 1572864 | tf_op jit(solution)/shard_map/all_gather | solution.py:39
  278.7 285.3 %all-gather.25.cloned.1.call-start = ((), (), s32[]{:S(2)}) async-start(), calls=%async_computation.13 | async-start | bytes 17825792 | tf_op jit(solution)/shard_map/all_gather | solution.py:126
  279.5 359.9 %all-gather.27.cloned.1.call-start = ((), (), s32[]{:S(2)}) async-start(), calls=%async_computation.14 | async-start | bytes 17825792 | tf_op jit(solution)/shard_map/all_gather | solution.py:127
  280.2 401.8 %reduce-scatter.11.cloned.1.call-start = ((), (), s32[]{:S(2)}) async-start(), calls=%async_computation.15 | async-start | bytes 3145728 | tf_op jit(solution)/shard_map/reduce_scatter | solution.py:43
  297.4 33.1 %collective-permute-start.8 = (bf16[128,4096]{1,0:T(8,128)(2,1)}, bf16[128,4096]{1,0:T(8,128)(2,1)S(1)}, u32[]{:S(2)}, u32[]{:S(2)}) collective-permute-start(bf16[128,4096]{1,0:T(8,128)(2,1)} %param.20), channel_id=1, source_target_pairs={{2,0},{4,2},{6,4},{8,6},{10,8},{12,10},{14,12},{16,14},{18,16},{20... | collective-permute-start | bytes 3145736 | tf_op jit(solution)/shard_map/ppermute | solution.py:27
  314.5 39.5 %collective-permute-start.2 = (bf16[128,4096]{1,0:T(8,128)(2,1)S(1)}, bf16[128,4096]{1,0:T(8,128)(2,1)S(1)}, u32[]{:S(2)}, u32[]{:S(2)}) collective-permute-start(bf16[128,4096]{1,0:T(8,128)(2,1)S(1)} %collective-permute-done.1), channel_id=1, source_target_pairs={{0,2},{2,4},{4,6},{6,8},{8,10},{10,12},{12,14},{14,16},{16,18},{18... | collective-permute-start | bytes 3145736 | tf_op jit(solution)/shard_map/ppermute | solution.py:25
  359.5 36.9 %collective-permute-start.10 = (bf16[128,4096]{1,0:T(8,128)(2,1)S(1)}, bf16[128,4096]{1,0:T(8,128)(2,1)S(1)}, u32[]{:S(2)}, u32[]{:S(2)}) collective-permute-start(bf16[128,4096]{1,0:T(8,128)(2,1)S(1)} %collective-permute-done.9), channel_id=1, source_target_pairs={{2,0},{4,2},{6,4},{8,6},{10,8},{12,10},{14,12},{16,14},{18,16},{20... | collective-permute-start | bytes 3145736 | tf_op jit(solution)/shard_map/ppermute | solution.py:27
  376.0 39.5 %collective-permute-start.4 = (bf16[128,4096]{1,0:T(8,128)(2,1)S(1)}, bf16[128,4096]{1,0:T(8,128)(2,1)S(1)}, u32[]{:S(2)}, u32[]{:S(2)}) collective-permute-start(bf16[128,4096]{1,0:T(8,128)(2,1)S(1)} %collective-permute-done.3), channel_id=1, source_target_pairs={{0,2},{2,4},{4,6},{6,8},{8,10},{10,12},{12,14},{14,16},{16,18},{18... | collective-permute-start | bytes 3145736 | tf_op jit(solution)/shard_map/ppermute | solution.py:25
  396.4 41.5 %collective-permute-start.11 = (bf16[128,4096]{1,0:T(8,128)(2,1)S(1)}, bf16[128,4096]{1,0:T(8,128)(2,1)S(1)}, u32[]{:S(2)}, u32[]{:S(2)}) collective-permute-start(bf16[128,4096]{1,0:T(8,128)(2,1)S(1)} %collective-permute-done.10), channel_id=1, source_target_pairs={{2,0},{4,2},{6,4},{8,6},{10,8},{12,10},{14,12},{16,14},{18,16},{20... | collective-permute-start | bytes 3145736 | tf_op jit(solution)/shard_map/ppermute | solution.py:27
  440.2 58.2 %collective-permute-start.6 = (bf16[128,4096]{1,0:T(8,128)(2,1)S(1)}, bf16[128,4096]{1,0:T(8,128)(2,1)}, u32[]{:S(2)}, u32[]{:S(2)}) collective-permute-start(bf16[128,4096]{1,0:T(8,128)(2,1)S(1)} %collective-permute-done.5), channel_id=1, source_target_pairs={{0,2},{2,4},{4,6},{6,8},{8,10},{10,12},{12,14},{14,16},{16,18},{18... | collective-permute-start | bytes 3145736 | tf_op jit(solution)/shard_map/ppermute | solution.py:25
  498.5 38.4 %collective-permute-start.14 = (bf16[128,4096]{1,0:T(8,128)(2,1)}, bf16[128,4096]{1,0:T(8,128)(2,1)S(1)}, u32[]{:S(2)}, u32[]{:S(2)}) collective-permute-start(bf16[128,4096]{1,0:T(8,128)(2,1)} %collective-permute-done.13), channel_id=1, source_target_pairs={{2,0},{4,2},{6,4},{8,6},{10,8},{12,10},{14,12},{16,14},{18,16},{20... | collective-permute-start | bytes 3145736 | tf_op jit(solution)/shard_map/ppermute | solution.py:27
  651.7 57.0 %all-gather.29.cloned.1.call-start = ((), (), s32[]{:S(2)}) async-start(), calls=%async_computation.16 | async-start | bytes 1572864 | tf_op jit(solution)/shard_map/all_gather | solution.py:39
  687.3 149.9 %all-gather.31.cloned.1.call-start = ((), (), s32[]{:S(2)}) async-start(), calls=%async_computation.17 | async-start | bytes 17825792 | tf_op jit(solution)/shard_map/all_gather | solution.py:150
  687.8 205.0 %reduce-scatter.13.cloned.1.call-start = ((), (), s32[]{:S(2)}) async-start(), calls=%async_computation.18 | async-start | bytes 3145728 | tf_op jit(solution)/shard_map/reduce_scatter | solution.py:43
  862.6 56.8 %all-gather.33.cloned.1.call-start = ((), (), s32[]{:S(2)}) async-start(), calls=%async_computation.19 | async-start | bytes 1572864 | tf_op jit(solution)/shard_map/all_gather | solution.py:39
  897.9 204.4 %reduce-scatter.19.cloned.1.call-start = ((), (), s32[]{:S(2)}) async-start(), calls=%async_computation.22 | async-start | bytes 1081344
  965.6 166.7 %reduce-scatter.15.cloned.1.call-start = ((), (), s32[]{:S(2)}) async-start(), calls=%async_computation.20 | async-start | bytes 3145728 | tf_op jit(solution)/shard_map/reduce_scatter | solution.py:43
  1009.3 1364.6 %reduce-scatter.17.cloned.1.call-start = ((), (), s32[]{:S(2)}) async-start(), calls=%async_computation.21 | async-start | bytes 142606336 | tf_op jit(solution)/shard_map/reduce_scatter | solution.py:227
  (59 other events, 1165.7 us)
Sparse Core Ops, SparseCore 0:
  9.5 24.2 all-gather.12
  36.0 50.3 all-gather.16
  88.6 48.9 all-gather.18
  139.6 48.8 all-gather.14
  190.6 48.8 all-gather.20
  244.6 30.4 reduce-scatter.8
  278.8 21.2 all-gather.22
  302.3 188.7 all-gather.24
  493.3 146.0 all-gather.26
  651.8 30.0 reduce-scatter.10
  687.4 21.2 all-gather.28
  710.7 126.4 all-gather.30
  862.7 30.0 reduce-scatter.12
  898.0 21.2 all-gather.32
  965.7 136.5 reduce-scatter.18
  1104.4 27.9 reduce-scatter.14
  1136.4 1237.4 reduce-scatter.16
